TPU v7x, 32 devices: a whole 2x2x4 slice. The times are simulated.
32 devices in a mesh: grp: 2 (over y), seg: 16 (over z, x, core).
Axes of the slice: x: 2, y: 2, z: 4, core: 2. Of those that a mesh axis runs over, the one named last changes fastest.
Arguments:
- strain: bfloat16 [524288], P(('grp', 'seg')), parts along dimension 0, may hold values from -6 to 6
- templates: bfloat16 [128, 512], P('seg'), may hold values from -6 to 6
Outputs:
- profile: float32 [32, 128], P(('grp', 'seg')), parts along dimension 0
- overall: float32 [256], P('grp'), parts along dimension 0
There are 2 independent parts, one for each index of `grp`. A program takes and returns all parts, laid end to end along the dimension named above; an argument that names none is the same for every part. Nothing has to cross between parts.
All inputs are finite; a program needn't handle non-finite values.
Results may differ from a plain program's by a relative error of at most 0.0003.
Values may be sent and summed in bfloat16 or wider, within the bound.
A program may use at most 256 MiB of HBM per device.

v0:
```python
import jax
import jax.numpy as jnp
from jax import lax
from jax.sharding import PartitionSpec as P

EPSILON = 1e-05


def passed_along(block, axis, distance):
    devices = range(lax.axis_size(axis))
    route = [(i - distance, i) for i in devices if i - distance in devices]
    return lax.ppermute(block, axis, route)


def hankel(extended, width):
    count = (extended.shape[0] - width) // width
    lower = extended[: count * width].reshape(count, width)
    upper = extended[width:].reshape(count, width)
    paired = jnp.concatenate([lower, upper], axis=1)
    tiled = jnp.tile(paired, (1, width + 1))[:, : width * (2 * width + 1)]
    windows = tiled.reshape(count, width, 2 * width + 1)[:, :, :width].reshape(count * width, width)
    return (paired, windows)


def window_stats(paired, width):
    rows = jnp.arange(2 * width)[:, None]
    cols = jnp.arange(width)[None, :]
    ones_band = ((rows >= cols) & (rows < cols + width)).astype(jnp.float32)
    floats = paired.astype(jnp.float32)
    totals = jnp.dot(floats, ones_band, precision=lax.Precision.HIGHEST).reshape(-1)
    squared = jnp.dot(floats * floats, ones_band, precision=lax.Precision.HIGHEST).reshape(-1)
    win_mean = totals / width
    variance = squared / width - win_mean * win_mean
    return (win_mean, jnp.sqrt(jnp.maximum(variance, 0.0) + EPSILON))


def template_minima(windows, win_mean, win_dev, usable, templates):
    width = templates.shape[1]
    floats = templates.astype(jnp.float32)
    t_mean = jnp.mean(floats, axis=1)
    t_dev = jnp.sqrt(jnp.mean((floats - t_mean[:, None]) ** 2, axis=1) + EPSILON)
    products = lax.dot_general(
        windows, templates, (((1,), (1,)), ((), ())), preferred_element_type=jnp.float32
    )
    rho = (products - width * win_mean[:, None] * t_mean[None, :]) / (
        width * win_dev[:, None] * t_dev[None, :]
    )
    distance = jnp.sqrt(jnp.maximum(2.0 - 2.0 * rho, 0.0))
    distance = jnp.where(usable[:, None], distance, jnp.inf)
    return jnp.min(distance, axis=0)


def per_device(strain, templates):
    width = templates.shape[1]
    seg_len = strain.shape[0]
    following = passed_along(strain[:width], "seg", -1)
    extended = jnp.concatenate([strain, following])
    paired, windows = hankel(extended, width)
    win_mean, win_dev = window_stats(paired, width)
    number = lax.axis_index("seg")
    places = number * seg_len + jnp.arange(seg_len, dtype=jnp.int32)
    usable = places <= seg_len * lax.axis_size("seg") - width
    gathered = lax.all_gather(templates, "seg", axis=0, tiled=True)
    minima = template_minima(windows, win_mean, win_dev, usable, gathered)
    profile = minima[None, :]
    collected = lax.all_gather(profile, "seg", axis=0, tiled=True)
    overall = jnp.min(collected, axis=0)
    return (profile, overall)


def solution(mesh):
    in_specs = (P(("grp", "seg")), P("seg", None))
    out_specs = (P(("grp", "seg"), None), P("grp"))
    return jax.shard_map(
        per_device, mesh=mesh, in_specs=in_specs, out_specs=out_specs, check_vma=False
    )
```

profile of v0, /device:TPU:0, one launch (start us, length us, event | category | flops | bytes accessed | tf_op | source)
XLA Modules:
  0.0 228.7 jit_solution(16680242244528655759)
XLA Ops:
  0.6 0.7 slice.22
  1.3 1.3 collective-permute-start
  2.6 0.8 reshape.71
  3.4 24.3 %all_gather.6 = bf16[128,512]{1,0:T(8,128)(2,1)S(1)} all-gather(bf16[8,512]{1,0:T(8,128)(2,1)} %param.3), channel_id=1, replica_groups=mesh['grp'=2,'seg'=16] {'seg'}, dimensions={0}, use_global_device_ids=true | all-gather | bytes 139264 | tf_op jit(solution)/shard_map/all_gather | solution.py:63
  27.7 0.1 convert_reduce_fusion
  27.9 0.2 fusion.24
  28.1 0.0 collective-permute-done
  28.1 0.8 pad_maximum_fusion
  28.9 0.5 fusion.12
  29.4 0.8 fusion.18
  30.3 11.3 %tile.4 = bf16[32,513,1024]{2,1,0:T(8,128)(2,1)} broadcast(bf16[32,1024]{1,0:T(8,128)(2,1)S(1)} %constant_dynamic-update-slice_fusion), dimensions={0,2} | broadcast | bytes 33685504 | tf_op jit(solution)/shard_map/tile | solution.py:20
  41.5 23.4 %copy.4 = bf16[4,8,513,1024]{3,1,2,0:T(8,128)(2,1)} copy(bf16[4,8,513,1024]{3,2,1,0:T(8,128)(2,1)} %bitcast.14) | data formatting | bytes 67239936
  64.9 22.9 %slice.27 = bf16[32,524800]{1,0:T(8,128)(2,1)} slice(bf16[32,525312]{1,0:T(8,128)(2,1)} %bitcast.15), slice={[0:32], [0:524800]} | slice | bytes 67174400 | tf_op jit(solution)/shard_map/slice | solution.py:20
  87.8 108.4 %reshape.72 = bf16[32,512,1025]{2,1,0:T(8,128)(2,1)} reshape(bf16[32,524800]{1,0:T(8,128)(2,1)} %slice.27) | data formatting | bytes 67174400 | tf_op jit(solution)/shard_map/reshape | solution.py:21
  196.2 0.0 slice-start
  196.3 5.7 %slice-done = bf16[32,512,512]{2,1,0:T(8,128)(2,1)S(1)} async-done(((bf16[32,512,1025]{2,1,0:T(8,128)(2,1)}), bf16[32,512,512]{2,1,0:T(8,128)(2,1)S(1)}, s32[]{:S(2)}) %slice-start) | async-done | bytes 16777240 | tf_op jit(solution)/shard_map/slice | solution.py:21
  202.0 8.7 %fusion.7 = f32[128]{0:T(128)S(1)} fusion(f32[128]{0:T(128)S(1)} %add_sqrt_fusion, f32[16384]{0:T(1024)S(1)} %sqrt_multiply_fusion, f32[128]{0:T(128)S(1)} %broadcast_multiply_fusion, f32[16384]{0:T(1024)S(1)} %bitcast.18, bf16[16384,512]{1,0:T(8,128)(2,1)S(1)} %bitcast.16, bf16[128,512]{1,0:T(8,128)(2,1)S(1)} %all_gather.6, ...), kind=kOutput, calls=%fused_computation.10 | convolution fusion | flops 2166358016 | bytes 17057280 | tf_op jit(solution)/shard_map/dot_general | solution.py:42
  210.7 0.0 copy-start
  210.7 17.4 %all-gather.1 = f32[16,1,128]{2,1,0:T(1,128)S(1)} all-gather(f32[1,1,128]{2,1,0:T(1,128)S(1)} %bitcast.20), channel_id=2, replica_groups=mesh['grp'=2,'seg'=16] {'seg'}, dimensions={0}, use_global_device_ids=true | all-gather | bytes 8704 | tf_op jit(solution)/shard_map/all_gather | solution.py:66
  228.2 0.5 reduce_min.19
  228.7 0.0 copy-done
  (10 shorter events, 0.1 us)
Async XLA Ops:
  1.3 26.8 %collective-permute-start = (bf16[512]{0:T(512)(128)(2,1)S(1)}, bf16[512]{0:T(512)(128)(2,1)S(1)}, u32[]{:S(2)}, u32[]{:S(2)}) collective-permute-start(bf16[512]{0:T(512)(128)(2,1)S(1)} %slice.22), channel_id=1, source_target_pairs={{1,0},{2,1},{3,2},{4,3},{5,4},{6,5},{7,6},{8,7},{9,8},{10,9},{11,1... | collective-permute-start | bytes 3080 | tf_op jit(solution)/shard_map/ppermute | solution.py:12
  196.2 5.8 %slice-start = ((bf16[32,512,1025]{2,1,0:T(8,128)(2,1)}), bf16[32,512,512]{2,1,0:T(8,128)(2,1)S(1)}, s32[]{:S(2)}) async-start(bf16[32,512,1025]{2,1,0:T(8,128)(2,1)} %reshape.72), calls=%async_computation | async-start | bytes 33554432 | tf_op jit(solution)/shard_map/slice | solution.py:21
  210.7 18.0 %copy-start = (f32[128]{0:T(128)}, f32[128]{0:T(128)S(1)}, u32[]{:S(2)}) copy-start(f32[128]{0:T(128)S(1)} %fusion.7) | copy-start | bytes 1540
where the time goes:
time: 229 us
  local copies, waits for them, and re-layouts  173 us (76%)
  blocking collectives  41.8 us (18%)
  matrix products  9.95 us (4%)
    reshape x1, local copies, waits for them, and re-layouts, hankel(): tiled.reshape(count, width, 2 * width + 1)[:, :, :width]  108 us
    all_gather x1, blocking collectives, per_device(): gathered = lax.all_gather(templates, 'seg', axis=0, tiled=True)  24.3 us
    unnamed x6, local copies, waits for them, and re-layouts  23.4 us
    slice x1, local copies, waits for them, and re-layouts, hankel(): tiled = jnp.tile(paired, (1, width + 1))[:, :width * (2 * width + 1)]  22.9 us
    all_gather x1, blocking collectives, per_device(): collected = lax.all_gather(profile, 'seg', axis=0, tiled=True)  17.4 us
    another operation x1, local copies, waits for them, and re-layouts, hankel(): tiled = jnp.tile(paired, (1, width + 1))[:, :width * (2 * width + 1)]  11.3 us
    dot_general x1, matrix products, template_minima(): lax.dot_general(windows, templates, (((1,), (1,)), ((), ())), preferred_e...  8.69 us
    slice x2, local copies, waits for them, and re-layouts, hankel(): tiled.reshape(count, width, 2 * width + 1)[:, :, :width]  5.73 us
  transfers between devices with their start and end apart: 1, of which 0 were waited for; matrix products, arithmetic and copies ran while one was open for 0% of the time, Pallas kernels for 0%

commit v1 on v0

v1 whole, which is shorter than its diff:
```python
import functools

import jax
import jax.numpy as jnp
from jax import lax
from jax.experimental import pallas as pl
from jax.experimental.pallas import tpu as pltpu
from jax.sharding import PartitionSpec as P

EPSILON = 1e-05
LANES = 128
SUBLANES = 8
PACKED = 16
MESH = pl.DeviceIdType.MESH


def each(count, body):
    if count <= 16:
        for step in range(count):
            body(step)
    else:
        lax.fori_loop(0, count, lambda step, _: (body(step), 0)[1], 0)


def largest_divisor(number, bound):
    return max(d for d in range(1, bound + 1) if number % d == 0)


def later(rows, samples):
    turned = pltpu.roll(rows, LANES - samples, 1)
    below = jnp.concatenate([turned[1:], turned[:1]], axis=0)
    lane = lax.broadcasted_iota(jnp.int32, rows.shape, 1)
    return jnp.where(lane < LANES - samples, turned, below)


def window_sums(rows, width):
    span = 1
    while span < LANES:
        rows = rows + later(rows, span)
        span *= 2
    while span < width:
        step = span // LANES
        rows = rows + jnp.concatenate([rows[step:], rows[:step]], axis=0)
        span *= 2
    return rows


def kernel(n, width, gathers, strain_ref, templates_ref, profile_ref, overall_ref,
           halo, gathered, near, hankel, sums, scales, minima, mine,
           halo_send, halo_recv, send, recv, out_send, out_recv):
    me = lax.axis_index("seg")
    grp = lax.axis_index("grp")
    rows = strain_ref.shape[0]
    extra = width // LANES
    tiles = rows + extra
    padded = near.shape[1] // LANES
    before = lax.rem(me + n - 1, n)

    def peer(step):
        return lax.rem(me + step + 1, n)

    barrier = pltpu.get_barrier_semaphore()
    each(n - 1, lambda step: pl.semaphore_signal(
        barrier, inc=1, device_id=(grp, peer(step)), device_id_type=MESH))

    def spread(values, first, count):
        for row in range(count):
            near[:, pl.ds((first + row) * LANES, LANES)] = jnp.broadcast_to(
                values[row : row + 1], (SUBLANES, LANES))

    def stagger(start, count):
        span = (count + 1) * LANES
        sub = lax.broadcasted_iota(jnp.int32, (SUBLANES, span), 0)
        base = near[:, pl.ds(start, span)]
        for bit in (1, 2, 4):
            base = jnp.where((sub & bit) != 0, pltpu.roll(base, span - bit, 1), base)
        for pair in range(LANES // PACKED):
            both = []
            for half in range(2):
                amount = pair * PACKED + half * SUBLANES
                turned = base if amount == 0 else pltpu.roll(base, span - amount, 1)
                both.append(turned[:, : count * LANES])
            hankel[pl.ds(pair * PACKED, PACKED), pl.ds(start, count * LANES)] = (
                jnp.concatenate(both, axis=0).astype(jnp.bfloat16))

    strain = strain_ref[...].astype(jnp.float32)
    spread(strain, 0, rows)
    early = rows - SUBLANES
    chunk = largest_divisor(early, 10)

    def build(step, _):
        stagger(pl.multiple_of(step * (chunk * LANES), LANES), chunk)
        return 0

    lax.fori_loop(0, early // chunk, build, 0)

    pl.semaphore_wait(barrier, n - 1)

    halo_copy = pltpu.make_async_remote_copy(
        src_ref=strain_ref.at[pl.ds(0, PACKED)], dst_ref=halo,
        send_sem=halo_send, recv_sem=halo_recv, device_id=(grp, before), device_id_type=MESH)
    halo_copy.start()

    def template_copy(step):
        return pltpu.make_async_remote_copy(
            src_ref=templates_ref, dst_ref=gathered.at[me],
            send_sem=send.at[step], recv_sem=recv.at[step],
            device_id=(grp, peer(step)), device_id_type=MESH)

    if gathers:
        each(n - 1, lambda step: template_copy(step).start())
        gathered[me] = templates_ref[...]

    halo_copy.wait()
    following = halo[...].astype(jnp.float32)
    following = jnp.where(me == n - 1, jnp.zeros_like(following), following)
    spread(following, rows, padded - rows)
    stagger(early * LANES, tiles - early)

    extended = jnp.concatenate([strain, following[:SUBLANES]], axis=0)
    totals = window_sums(extended, width)[:rows]
    squared = window_sums(extended * extended, width)[:rows]
    win_mean = totals / width
    win_dev = jnp.sqrt(jnp.maximum(squared / width - win_mean * win_mean, 0.0) + EPSILON)
    sums[...] = totals
    scales[...] = 1.0 / win_dev

    if gathers:
        each(n - 1, lambda step: template_copy(step).wait())
        floats = gathered[...].astype(jnp.float32).reshape(-1, width)
    else:
        floats = templates_ref[...].astype(jnp.float32)
    templates = floats.astype(jnp.bfloat16)
    queries = floats.shape[0]
    t_mean = jnp.mean(floats, axis=1, keepdims=True)
    t_dev = jnp.sqrt(jnp.mean((floats - t_mean) ** 2, axis=1, keepdims=True) + EPSILON)
    t_wide = jnp.broadcast_to(t_mean, (queries, LANES))

    def scores(tile, count):
        block = jnp.concatenate(
            [hankel[:, pl.ds(pl.multiple_of((tile + c) * LANES, LANES), count * LANES)]
             for c in range(extra)], axis=0)
        products = jnp.dot(templates, block, preferred_element_type=jnp.float32)
        return [
            (products[:, h * LANES : (h + 1) * LANES] - sums[pl.ds(tile + h, 1), :] * t_wide)
            * scales[pl.ds(tile + h, 1), :]
            for h in range(count)
        ]

    pairs = (rows - extra) // 2

    def fold(step, best):
        one, two = scores(step * 2, 2)
        return jnp.maximum(best, jnp.maximum(one, two))

    best = lax.fori_loop(0, pairs, fold, jnp.full((queries, LANES), -jnp.inf, jnp.float32))
    lane = lax.broadcasted_iota(jnp.int32, (1, LANES), 1)
    for tile in range(2 * pairs, rows, 2):
        for h, score in enumerate(scores(tile, 2)):
            last = (tile + h) * LANES + lane
            usable = (me < n - 1) | (last <= rows * LANES - width)
            best = jnp.maximum(best, jnp.where(usable, score, -jnp.inf))
    best = best / (width * t_dev)
    rho = jnp.max(best.T, axis=0, keepdims=True)
    distance = jnp.sqrt(jnp.maximum(2.0 - 2.0 * rho, 0.0))
    profile_ref[...] = distance
    mine[...] = distance
    minima[me] = distance

    def out_copy(step):
        return pltpu.make_async_remote_copy(
            src_ref=mine, dst_ref=minima.at[me],
            send_sem=out_send.at[step], recv_sem=out_recv.at[step],
            device_id=(grp, peer(step)), device_id_type=MESH)

    each(n - 1, lambda step: out_copy(step).start())
    each(n - 1, lambda step: out_copy(step).wait())
    overall_ref[...] = jnp.min(minima[...], axis=0)


def per_device(n, strain, templates):
    width = templates.shape[1]
    held = templates.shape[0]
    queries = n * held
    gathers = held % SUBLANES == 0
    if not gathers:
        templates = lax.all_gather(templates, "seg", axis=0, tiled=True)
    rows = strain.shape[0] // LANES
    extra = width // LANES
    padded = rows + SUBLANES
    dma = pltpu.SemaphoreType.DMA
    vmem = pl.BlockSpec(memory_space=pltpu.VMEM)
    profile, overall = pl.pallas_call(
        functools.partial(kernel, n, width, gathers),
        out_shape=[jax.ShapeDtypeStruct((1, queries), jnp.float32)] * 2,
        in_specs=[vmem] * 2,
        out_specs=[vmem] * 2,
        scratch_shapes=[
            pltpu.VMEM((PACKED, LANES), jnp.bfloat16),
            pltpu.VMEM((n, max(held, SUBLANES), width), jnp.bfloat16),
            pltpu.VMEM((SUBLANES, padded * LANES), jnp.float32),
            pltpu.VMEM((LANES, (rows + extra) * LANES), jnp.bfloat16),
            pltpu.VMEM((rows, LANES), jnp.float32),
            pltpu.VMEM((rows, LANES), jnp.float32),
            pltpu.VMEM((n, 1, queries), jnp.float32),
            pltpu.VMEM((1, queries), jnp.float32),
            dma, dma, dma((n - 1,)), dma((n - 1,)), dma((n - 1,)), dma((n - 1,)),
        ],
        compiler_params=pltpu.CompilerParams(collective_id=0, has_side_effects=True),
    )(strain.reshape(rows, LANES), templates)
    return (profile, overall.reshape(-1))


def solution(mesh):
    in_specs = (P(("grp", "seg")), P("seg", None))
    out_specs = (P(("grp", "seg"), None), P("grp"))
    return jax.shard_map(
        functools.partial(per_device, mesh.shape["seg"]),
        mesh=mesh, in_specs=in_specs, out_specs=out_specs, check_vma=False,
    )
```

time: 229 us -> 33.4 us (0.15)
  local copies, waits for them, and re-layouts: 173 us -> 1.8 us
  blocking collectives: 41.8 us -> 0 us
  Pallas kernels: 0 us -> 30.8 us
  matrix products: 9.95 us -> 0 us
    reshape x2 -> x0, local copies, waits for them, and re-layouts: 109 us -> none  [the longest x1 108 us: hankel(): tiled.reshape(count, width, 2 * width + 1)[:, :, :width]]
    all_gather x2 -> x0, blocking collectives: 41.8 us -> none  [the longest x1 24.3 us: per_device(): gathered = lax.all_gather(templates, 'seg', axis=0, tiled=True)]
    pallas_call x0 -> x1, Pallas kernels: none -> 30.8 us  [per_device(): pl.pallas_call(functools.partial(kernel, n, width, gathers), out_shape=[j...]
    slice x5 -> x0, local copies, waits for them, and re-layouts: 29.4 us -> none  [the longest x1 22.9 us: hankel(): tiled = jnp.tile(paired, (1, width + 1))[:, :width * (2 * width + 1)]]
    unnamed x6, local copies, waits for them, and re-layouts: 23.4 us -> 1.8 us
    another operation x1 -> x0, local copies, waits for them, and re-layouts: 11.3 us -> none  [hankel(): tiled = jnp.tile(paired, (1, width + 1))[:, :width * (2 * width + 1)]]
    dot_general x3 -> x0, matrix products: 9.95 us -> none  [the longest x1 8.69 us: template_minima(): lax.dot_general(windows, templates, (((1,), (1,)), ((), ())), preferred_e...]
  transfers between devices with their start and end apart: 1 -> 0, of which waited for: 0 -> 0; matrix products, arithmetic and copies ran while one was open for 0% -> 0% of each run, Pallas kernels for 0% -> 0%
where the time goes in v1:
time: 33.4 us; the launch traced here: 33.2 us
  Pallas kernels  30.8 us (92%)
  local copies, waits for them, and re-layouts  1.8 us (5%)
  between operations  0.65 us (2%)
    pallas_call x1, Pallas kernels, per_device(): pl.pallas_call(functools.partial(kernel, n, width, gathers), out_shape=[j...  30.8 us
    unnamed x6, local copies, waits for them, and re-layouts  1.8 us

profile of v1, /device:TPU:0, one launch (start us, length us, event | category | flops | bytes accessed | tf_op | source)
XLA Modules:
  0.0 33.2 jit_solution(12849853430986092329)
XLA Ops:
  0.6 30.8 %shard_map.41 = (f32[1,128]{1,0:T(1,128)}, f32[1,128]{1,0:T(1,128)}) custom-call(bf16[128,128]{1,0:T(8,128)(2,1)} %bitcast.2, bf16[8,512]{1,0:T(8,128)(2,1)} %templates_ref.1), custom_call_target="tpu_custom_call" | custom-call | tf_op jit(solution)/shard_map/pallas_call | solution.py:193
  31.4 0.0 copy-start.1
  31.4 0.7 %copy-done.1 = f32[1,128]{1,0:T(1,128)S(1)} copy-done((f32[1,128]{1,0:T(1,128)S(1)}, f32[1,128]{1,0:T(1,128)}, u32[]{:S(2)}) %copy-start.1) | copy-done | bytes 536
  32.1 0.0 copy-start
  32.1 0.5 %copy.6 = f32[1,128]{1,0:T(1,128)} copy(f32[1,128]{1,0:T(1,128)S(1)} %copy-done.1) | data formatting | bytes 1024
  32.6 0.1 copy-done
  32.7 0.5 %copy.7 = f32[128]{0:T(128)} copy(f32[128]{0:T(128)S(1)} %bitcast.3) | data formatting | bytes 1024
Async XLA Ops:
  31.4 0.7 %copy-start.1 = (f32[1,128]{1,0:T(1,128)S(1)}, f32[1,128]{1,0:T(1,128)}, u32[]{:S(2)}) copy-start(f32[1,128]{1,0:T(1,128)} %get-tuple-element.8) | copy-start | bytes 1540
  32.1 0.6 %copy-start = (f32[1,128]{1,0:T(1,128)S(1)}, f32[1,128]{1,0:T(1,128)}, u32[]{:S(2)}) copy-start(f32[1,128]{1,0:T(1,128)} %get-tuple-element.5) | copy-start | bytes 1540

commit v2 on v1

--- a/solution.py
+++ b/solution.py
@@ -11,6 +11,8 @@
 LANES = 128
 SUBLANES = 8
 PACKED = 16
+BATCH = 40
+GROUP = 4
 MESH = pl.DeviceIdType.MESH
 
 
@@ -31,6 +33,10 @@
     below = jnp.concatenate([turned[1:], turned[:1]], axis=0)
     lane = lax.broadcasted_iota(jnp.int32, rows.shape, 1)
     return jnp.where(lane < LANES - samples, turned, below)
+
+
+def largest_multiple(number, of):
+    return number // of * of
 
 
 def window_sums(rows, width):
@@ -147,19 +153,28 @@
             for h in range(count)
         ]
 
-    pairs = (rows - extra) // 2
-
-    def fold(step, best):
-        one, two = scores(step * 2, 2)
-        return jnp.maximum(best, jnp.maximum(one, two))
-
-    best = lax.fori_loop(0, pairs, fold, jnp.full((queries, LANES), -jnp.inf, jnp.float32))
+    def fold(start, count, best):
+        for score in scores(start, count):
+            best = jnp.maximum(best, score)
+        return best
+
+    main = largest_multiple(rows - extra, BATCH)
+
+    def batch(step, best):
+        for part in range(BATCH // GROUP):
+            best = fold(step * BATCH + part * GROUP, GROUP, best)
+        return best
+
+    best = lax.fori_loop(
+        0, main // BATCH, batch, jnp.full((queries, LANES), -jnp.inf, jnp.float32))
     lane = lax.broadcasted_iota(jnp.int32, (1, LANES), 1)
-    for tile in range(2 * pairs, rows, 2):
+    for tile in range(main, rows, 2):
         for h, score in enumerate(scores(tile, 2)):
-            last = (tile + h) * LANES + lane
-            usable = (me < n - 1) | (last <= rows * LANES - width)
-            best = jnp.maximum(best, jnp.where(usable, score, -jnp.inf))
+            if tile + h >= rows - extra:
+                last = (tile + h) * LANES + lane
+                usable = (me < n - 1) | (last <= rows * LANES - width)
+                score = jnp.where(usable, score, -jnp.inf)
+            best = jnp.maximum(best, score)
     best = best / (width * t_dev)
     rho = jnp.max(best.T, axis=0, keepdims=True)
     distance = jnp.sqrt(jnp.maximum(2.0 - 2.0 * rho, 0.0))

time: 33.4 us -> 24.2 us (0.72)
  Pallas kernels: 30.8 us -> 21.5 us
    pallas_call x1, Pallas kernels: 30.8 us -> 21.5 us  [per_device(): pl.pallas_call(functools.partial(kernel, n, width, gathers), out_shape=[j...]
where the time goes in v2:
time: 24.2 us; the launch traced here: 24 us
  Pallas kernels  21.5 us (89%)
  local copies, waits for them, and re-layouts  1.8 us (7%)
  between operations  0.65 us (3%)
    pallas_call x1, Pallas kernels, per_device(): pl.pallas_call(functools.partial(kernel, n, width, gathers), out_shape=[j...  21.5 us
    unnamed x6, local copies, waits for them, and re-layouts  1.8 us

profile of v2, /device:TPU:0, one launch (start us, length us, event | category | flops | bytes accessed | tf_op | source)
XLA Modules:
  0.0 24.0 jit_solution(15310941435918565082)
XLA Ops:
  0.6 21.5 %shard_map.41 = (f32[1,128]{1,0:T(1,128)}, f32[1,128]{1,0:T(1,128)}) custom-call(bf16[128,128]{1,0:T(8,128)(2,1)} %bitcast.2, bf16[8,512]{1,0:T(8,128)(2,1)} %templates_ref.1), custom_call_target="tpu_custom_call" | custom-call | tf_op jit(solution)/shard_map/pallas_call | solution.py:208
  22.2 0.0 copy-start.1
  22.2 0.7 %copy-done.1 = f32[1,128]{1,0:T(1,128)S(1)} copy-done((f32[1,128]{1,0:T(1,128)S(1)}, f32[1,128]{1,0:T(1,128)}, u32[]{:S(2)}) %copy-start.1) | copy-done | bytes 536
  22.9 0.0 copy-start
  22.9 0.5 %copy.6 = f32[1,128]{1,0:T(1,128)} copy(f32[1,128]{1,0:T(1,128)S(1)} %copy-done.1) | data formatting | bytes 1024
  23.4 0.1 copy-done
  23.5 0.5 %copy.7 = f32[128]{0:T(128)} copy(f32[128]{0:T(128)S(1)} %bitcast.3) | data formatting | bytes 1024
Async XLA Ops:
  22.2 0.7 %copy-start.1 = (f32[1,128]{1,0:T(1,128)S(1)}, f32[1,128]{1,0:T(1,128)}, u32[]{:S(2)}) copy-start(f32[1,128]{1,0:T(1,128)} %get-tuple-element.8) | copy-start | bytes 1540
  22.9 0.6 %copy-start = (f32[1,128]{1,0:T(1,128)S(1)}, f32[1,128]{1,0:T(1,128)}, u32[]{:S(2)}) copy-start(f32[1,128]{1,0:T(1,128)} %get-tuple-element.5) | copy-start | bytes 1540

commit v3 on v2

--- a/solution.py
+++ b/solution.py
@@ -13,6 +13,7 @@
 PACKED = 16
 BATCH = 40
 GROUP = 4
+AHEAD = 3
 MESH = pl.DeviceIdType.MESH
 
 
@@ -51,9 +52,9 @@
     return rows
 
 
-def kernel(n, width, gathers, strain_ref, templates_ref, profile_ref, overall_ref,
-           halo, gathered, near, hankel, sums, scales, minima, mine,
-           halo_send, halo_recv, send, recv, out_send, out_recv):
+def kernel(n, width, gathers, strain_any, templates_any, profile_ref, overall_ref,
+           strain_ref, templates_ref, halo, gathered, near, hankel, sums, scales, minima, mine,
+           local, halo_send, halo_recv, send, recv, out_send, out_recv):
     me = lax.axis_index("seg")
     grp = lax.axis_index("grp")
     rows = strain_ref.shape[0]
@@ -65,6 +66,12 @@
     def peer(step):
         return lax.rem(me + step + 1, n)
 
+    fetches = [
+        pltpu.make_async_copy(strain_any, strain_ref, local.at[0]),
+        pltpu.make_async_copy(templates_any, templates_ref, local.at[1]),
+    ]
+    for fetch in fetches:
+        fetch.start()
     barrier = pltpu.get_barrier_semaphore()
     each(n - 1, lambda step: pl.semaphore_signal(
         barrier, inc=1, device_id=(grp, peer(step)), device_id_type=MESH))
@@ -89,6 +96,8 @@
             hankel[pl.ds(pair * PACKED, PACKED), pl.ds(start, count * LANES)] = (
                 jnp.concatenate(both, axis=0).astype(jnp.bfloat16))
 
+    for fetch in fetches:
+        fetch.wait()
     strain = strain_ref[...].astype(jnp.float32)
     spread(strain, 0, rows)
     early = rows - SUBLANES
@@ -98,7 +107,9 @@
         stagger(pl.multiple_of(step * (chunk * LANES), LANES), chunk)
         return 0
 
-    lax.fori_loop(0, early // chunk, build, 0)
+    steps = early // chunk
+    ahead = steps // AHEAD
+    lax.fori_loop(0, ahead, build, 0)
 
     pl.semaphore_wait(barrier, n - 1)
 
@@ -117,6 +128,7 @@
         each(n - 1, lambda step: template_copy(step).start())
         gathered[me] = templates_ref[...]
 
+    lax.fori_loop(ahead, steps, build, 0)
     halo_copy.wait()
     following = halo[...].astype(jnp.float32)
     following = jnp.where(me == n - 1, jnp.zeros_like(following), following)
@@ -207,10 +219,12 @@
     vmem = pl.BlockSpec(memory_space=pltpu.VMEM)
     profile, overall = pl.pallas_call(
         functools.partial(kernel, n, width, gathers),
-        out_shape=[jax.ShapeDtypeStruct((1, queries), jnp.float32)] * 2,
-        in_specs=[vmem] * 2,
+        out_shape=[pltpu.VMEM((1, queries), jnp.float32)] * 2,
+        in_specs=[pl.BlockSpec(memory_space=pl.ANY)] * 2,
         out_specs=[vmem] * 2,
         scratch_shapes=[
+            pltpu.VMEM((rows, LANES), jnp.bfloat16),
+            pltpu.VMEM(templates.shape, jnp.bfloat16),
             pltpu.VMEM((PACKED, LANES), jnp.bfloat16),
             pltpu.VMEM((n, max(held, SUBLANES), width), jnp.bfloat16),
             pltpu.VMEM((SUBLANES, padded * LANES), jnp.float32),
@@ -219,7 +233,7 @@
             pltpu.VMEM((rows, LANES), jnp.float32),
             pltpu.VMEM((n, 1, queries), jnp.float32),
             pltpu.VMEM((1, queries), jnp.float32),
-            dma, dma, dma((n - 1,)), dma((n - 1,)), dma((n - 1,)), dma((n - 1,)),
+            dma((2,)), dma, dma, dma((n - 1,)), dma((n - 1,)), dma((n - 1,)), dma((n - 1,)),
         ],
         compiler_params=pltpu.CompilerParams(collective_id=0, has_side_effects=True),
     )(strain.reshape(rows, LANES), templates)

time: 24.2 us -> 21.4 us (0.88)
  Pallas kernels: 21.5 us -> 19.5 us
  local copies, waits for them, and re-layouts: 1.8 us -> 1.02 us
    pallas_call x1, Pallas kernels: 21.5 us -> 19.5 us  [per_device(): pl.pallas_call(functools.partial(kernel, n, width, gathers), out_shape=[p...]
    unnamed x6 -> x2, local copies, waits for them, and re-layouts: 1.8 us -> 1.02 us
where the time goes in v3:
time: 21.4 us; the launch traced here: 21.2 us
  Pallas kernels  19.5 us (91%)
  local copies, waits for them, and re-layouts  1.02 us (5%)
  between operations  0.64 us (3%)
    pallas_call x1, Pallas kernels, per_device(): pl.pallas_call(functools.partial(kernel, n, width, gathers), out_shape=[p...  19.5 us
    unnamed x2, local copies, waits for them, and re-layouts  1.02 us

profile of v3, /device:TPU:0, one launch (start us, length us, event | category | flops | bytes accessed | tf_op | source)
XLA Modules:
  0.0 21.2 jit_solution(11491247834771063002)
XLA Ops:
  0.6 19.5 %shard_map.41 = (f32[1,128]{1,0:T(1,128)S(1)}, f32[1,128]{1,0:T(1,128)S(1)}) custom-call(bf16[128,128]{1,0:T(8,128)(2,1)} %bitcast.3, bf16[8,512]{1,0:T(8,128)(2,1)} %templates_any.1), custom_call_target="tpu_custom_call" | custom-call | tf_op jit(solution)/shard_map/pallas_call | solution.py:220
  20.2 0.5 %copy.6 = f32[1,128]{1,0:T(1,128)} copy(f32[1,128]{1,0:T(1,128)S(1)} %get-tuple-element.6) | data formatting | bytes 1024
  20.7 0.5 %copy.7 = f32[128]{0:T(128)} copy(f32[128]{0:T(128)S(1)} %bitcast.2) | data formatting | bytes 1024

commit v4 on v3

v4 whole, which is shorter than its diff:
```python
import functools

import jax
import jax.numpy as jnp
from jax import lax
from jax.experimental import pallas as pl
from jax.experimental.pallas import tpu as pltpu
from jax.sharding import PartitionSpec as P

EPSILON = 1e-05
LANES = 128
SUBLANES = 8
PACKED = 16
BATCH = 40
GROUP = 4
AHEAD = 3
CHUNK = 10
MESH = pl.DeviceIdType.MESH


def each(count, body):
    if count <= 16:
        for step in range(count):
            body(step)
    else:
        lax.fori_loop(0, count, lambda step, _: (body(step), 0)[1], 0)


def largest_divisor(number, bound):
    return max(d for d in range(1, bound + 1) if number % d == 0)


def largest_multiple(number, of):
    return number // of * of


def window_sums(parts, work, rows, extra):
    source = lax.broadcasted_iota(jnp.int32, (LANES, 2 * LANES), 0)
    place = lax.broadcasted_iota(jnp.int32, (LANES, 2 * LANES), 1)
    from_place = (place < LANES) & (source >= place)
    to_place = (place >= LANES) & (source < place - LANES)
    ones = jnp.where(from_place | to_place, 1.0, 0.0).astype(jnp.bfloat16)
    both = sum(jnp.dot(part, ones, preferred_element_type=jnp.float32) for part in parts)
    first, last = both[:, :LANES], both[:, LANES:]
    work[0] = first + last
    work[1] = last
    total = first[:rows]
    for row in range(1, extra):
        total = total + work[0, pl.ds(row, rows), :]
    return total + work[1, pl.ds(extra, rows), :]


def kernel(n, width, gathers, strain_any, templates_any, profile_ref, overall_ref,
           strain_ref, templates_ref, halo, gathered, longer, work, near, hankel, sums, scales, minima, mine,
           local, halo_send, halo_recv, send, recv, out_send, out_recv):
    me = lax.axis_index("seg")
    grp = lax.axis_index("grp")
    rows = strain_ref.shape[0]
    extra = width // LANES
    tiles = rows + extra
    before = lax.rem(me + n - 1, n)

    def peer(step):
        down = n - 1 - step
        down = jnp.where(down <= me, down - 1, down)
        up = jnp.where(step >= me, step + 1, step)
        return jnp.where(me * 2 < n, down, up)

    fetches = [
        pltpu.make_async_copy(strain_any, strain_ref, local.at[0]),
        pltpu.make_async_copy(templates_any, templates_ref, local.at[1]),
    ]
    for fetch in fetches:
        fetch.start()
    def other(step):
        return jnp.where(step >= me, step + 1, step)

    barrier = pltpu.get_barrier_semaphore()
    each(n - 1, lambda step: pl.semaphore_signal(
        barrier, inc=1, device_id=(grp, peer(step)), device_id_type=MESH))

    def spread(first, count):
        lane = lax.broadcasted_iota(jnp.int32, (count, LANES), 1)
        here = longer[pl.ds(first, count), :]
        below = longer[pl.ds(first + 1, count), :]
        near[pl.ds(first, count), 0, :] = here
        for shift in range(1, PACKED):
            near[pl.ds(first, count), shift, :] = pltpu.roll(
                jnp.where(lane >= shift, here, below), LANES - shift, 1)

    def stagger(first, count):
        span = (count + 1) * LANES
        tiles = near[pl.ds(first, count + 1)].astype(jnp.bfloat16)
        base = jnp.concatenate([tiles[i] for i in range(count + 1)], axis=1)
        start = pl.multiple_of(first * LANES, LANES)
        for group in range(LANES // PACKED):
            turned = base if group == 0 else pltpu.roll(base, span - group * PACKED, 1)
            hankel[pl.ds(group * PACKED, PACKED), pl.ds(start, count * LANES)] = (
                turned[:, : count * LANES])

    for fetch in fetches:
        fetch.wait()
    longer[pl.ds(0, rows), :] = strain_ref[...].astype(jnp.float32)
    longer[pl.ds(rows, PACKED), :] = jnp.zeros((PACKED, LANES), jnp.float32)
    spread(0, rows)
    early = rows - SUBLANES
    chunk = largest_divisor(early, CHUNK)

    def build(step, _):
        stagger(step * chunk, chunk)
        return 0

    steps = early // chunk
    ahead = steps // AHEAD
    lax.fori_loop(0, ahead, build, 0)

    pl.semaphore_wait(barrier, n - 1)

    halo_copy = pltpu.make_async_remote_copy(
        src_ref=strain_ref.at[pl.ds(0, PACKED)], dst_ref=halo,
        send_sem=halo_send, recv_sem=halo_recv, device_id=(grp, before), device_id_type=MESH)
    halo_copy.start()

    def template_copy(step):
        return pltpu.make_async_remote_copy(
            src_ref=templates_ref, dst_ref=gathered.at[me],
            send_sem=send.at[step], recv_sem=recv.at[me],
            device_id=(grp, peer(step)), device_id_type=MESH)

    def template_arrival(sender):
        return pltpu.make_async_remote_copy(
            src_ref=templates_ref, dst_ref=gathered.at[sender],
            send_sem=send.at[0], recv_sem=recv.at[sender],
            device_id=(grp, sender), device_id_type=MESH)

    if gathers:
        each(n - 1, lambda step: template_copy(step).start())
        gathered[me] = templates_ref[...]

    lax.fori_loop(ahead, steps, build, 0)
    halo_copy.wait()
    following = halo[...].astype(jnp.float32)
    following = jnp.where(me == n - 1, jnp.zeros_like(following), following)
    longer[pl.ds(rows, PACKED), :] = following
    spread(early, PACKED)
    stagger(early, tiles - early)

    extended = longer[...]
    square = extended * extended
    high = square.astype(jnp.bfloat16)
    low = (square - high.astype(jnp.float32)).astype(jnp.bfloat16)
    totals = window_sums([extended.astype(jnp.bfloat16)], work.at[0], rows, extra)
    squared = window_sums([high, low], work.at[1], rows, extra)
    win_mean = totals / width
    win_dev = jnp.sqrt(jnp.maximum(squared / width - win_mean * win_mean, 0.0) + EPSILON)
    sums[...] = totals
    scales[...] = 1.0 / win_dev

    def scores(templates, t_wide, tile, count):
        block = jnp.concatenate(
            [hankel[:, pl.ds(pl.multiple_of((tile + c) * LANES, LANES), count * LANES)]
             for c in range(extra)], axis=0)
        products = jnp.dot(templates, block, preferred_element_type=jnp.float32)
        return [
            (products[:, h * LANES : (h + 1) * LANES] - sums[pl.ds(tile + h, 1), :] * t_wide)
            * scales[pl.ds(tile + h, 1), :]
            for h in range(count)
        ]

    main = largest_multiple(rows - extra, BATCH)
    lane = lax.broadcasted_iota(jnp.int32, (1, LANES), 1)

    def largest_rho(floats):
        templates = floats.astype(jnp.bfloat16)
        queries = floats.shape[0]
        t_mean = jnp.mean(floats, axis=1, keepdims=True)
        t_dev = jnp.sqrt(jnp.mean((floats - t_mean) ** 2, axis=1, keepdims=True) + EPSILON)
        t_wide = jnp.broadcast_to(t_mean, (queries, LANES))

        def batch(step, best):
            for part in range(BATCH // GROUP):
                for score in scores(templates, t_wide, step * BATCH + part * GROUP, GROUP):
                    best = jnp.maximum(best, score)
            return best

        best = lax.fori_loop(
            0, main // BATCH, batch, jnp.full((queries, LANES), -jnp.inf, jnp.float32))
        for tile in range(main, rows, 2):
            for h, score in enumerate(scores(templates, t_wide, tile, 2)):
                if tile + h >= rows - extra:
                    last = (tile + h) * LANES + lane
                    usable = (me < n - 1) | (last <= rows * LANES - width)
                    score = jnp.where(usable, score, -jnp.inf)
                best = jnp.maximum(best, score)
        return best / (width * t_dev)

    if gathers:
        each(n - 1, lambda step: template_arrival(other(step)).wait_recv())
        best = largest_rho(gathered[...].astype(jnp.float32).reshape(-1, width))
    else:
        best = largest_rho(templates_ref[...].astype(jnp.float32))
    if gathers:
        each(n - 1, lambda step: template_copy(step).wait_send())
    rho = jnp.max(best.T, axis=0, keepdims=True)
    distance = jnp.sqrt(jnp.maximum(2.0 - 2.0 * rho, 0.0))
    profile_ref[...] = distance
    mine[...] = distance
    minima[me] = distance

    def out_copy(step):
        return pltpu.make_async_remote_copy(
            src_ref=mine, dst_ref=minima.at[me],
            send_sem=out_send.at[step], recv_sem=out_recv.at[me],
            device_id=(grp, peer(step)), device_id_type=MESH)

    def out_arrival(sender):
        return pltpu.make_async_remote_copy(
            src_ref=mine, dst_ref=minima.at[sender],
            send_sem=out_send.at[0], recv_sem=out_recv.at[sender],
            device_id=(grp, sender), device_id_type=MESH)

    each(n - 1, lambda step: out_copy(step).start())
    each(n - 1, lambda step: out_arrival(other(step)).wait_recv())
    each(n - 1, lambda step: out_copy(step).wait_send())
    overall_ref[...] = jnp.min(minima[...], axis=0)


def per_device(n, strain, templates):
    width = templates.shape[1]
    held = templates.shape[0]
    queries = n * held
    gathers = held % SUBLANES == 0
    if not gathers:
        templates = lax.all_gather(templates, "seg", axis=0, tiled=True)
    rows = strain.shape[0] // LANES
    extra = width // LANES
    dma = pltpu.SemaphoreType.DMA
    vmem = pl.BlockSpec(memory_space=pltpu.VMEM)
    profile, overall = pl.pallas_call(
        functools.partial(kernel, n, width, gathers),
        out_shape=[pltpu.VMEM((1, queries), jnp.float32)] * 2,
        in_specs=[pl.BlockSpec(memory_space=pl.ANY)] * 2,
        out_specs=[vmem] * 2,
        scratch_shapes=[
            pltpu.VMEM((rows, LANES), jnp.bfloat16),
            pltpu.VMEM(templates.shape, jnp.bfloat16),
            pltpu.VMEM((PACKED, LANES), jnp.bfloat16),
            pltpu.VMEM((n, max(held, SUBLANES), width), jnp.bfloat16),
            pltpu.VMEM((rows + PACKED, LANES), jnp.float32),
            pltpu.VMEM((2, 2, rows + PACKED, LANES), jnp.float32),
            pltpu.VMEM((rows + SUBLANES, PACKED, LANES), jnp.float32),
            pltpu.VMEM((LANES, (rows + extra) * LANES), jnp.bfloat16),
            pltpu.VMEM((rows, LANES), jnp.float32),
            pltpu.VMEM((rows, LANES), jnp.float32),
            pltpu.VMEM((n, 1, queries), jnp.float32),
            pltpu.VMEM((1, queries), jnp.float32),
            dma((2,)), dma, dma, dma((n - 1,)), dma((n,)), dma((n - 1,)), dma((n,)),
        ],
        compiler_params=pltpu.CompilerParams(collective_id=0, has_side_effects=True),
    )(strain.reshape(rows, LANES), templates)
    return (profile, overall.reshape(-1))


def solution(mesh):
    in_specs = (P(("grp", "seg")), P("seg", None))
    out_specs = (P(("grp", "seg"), None), P("grp"))
    return jax.shard_map(
        functools.partial(per_device, mesh.shape["seg"]),
        mesh=mesh, in_specs=in_specs, out_specs=out_specs, check_vma=False,
    )
```

time: 21.4 us -> 20.5 us (0.958)
  Pallas kernels: 19.5 us -> 18.6 us
    pallas_call x1, Pallas kernels: 19.5 us -> 18.6 us  [per_device(): pl.pallas_call(functools.partial(kernel, n, width, gathers), out_shape=[p...]
where the time goes in v4:
time: 20.5 us; the launch traced here: 20.3 us
  Pallas kernels  18.6 us (91%)
  local copies, waits for them, and re-layouts  1.02 us (5%)
  between operations  0.64 us (3%)
    pallas_call x1, Pallas kernels, per_device(): pl.pallas_call(functools.partial(kernel, n, width, gathers), out_shape=[p...  18.6 us
    unnamed x2, local copies, waits for them, and re-layouts  1.02 us

profile of v4, /device:TPU:0, one launch (start us, length us, event | category | flops | bytes accessed | tf_op | source)
XLA Modules:
  0.0 20.3 jit_solution(16135724154855495199)
XLA Ops:
  0.6 18.6 %shard_map.41 = (f32[1,128]{1,0:T(1,128)S(1)}, f32[1,128]{1,0:T(1,128)S(1)}) custom-call(bf16[128,128]{1,0:T(8,128)(2,1)} %bitcast.3, bf16[8,512]{1,0:T(8,128)(2,1)} %templates_any.1), custom_call_target="tpu_custom_call" | custom-call | tf_op jit(solution)/shard_map/pallas_call | solution.py:239
  19.2 0.5 %copy.6 = f32[1,128]{1,0:T(1,128)} copy(f32[1,128]{1,0:T(1,128)S(1)} %get-tuple-element.6) | data formatting | bytes 1024
  19.8 0.5 %copy.7 = f32[128]{0:T(128)} copy(f32[128]{0:T(128)S(1)} %bitcast.2) | data formatting | bytes 1024

commit v5 on v4

--- a/solution.py
+++ b/solution.py
@@ -11,7 +11,7 @@
 LANES = 128
 SUBLANES = 8
 PACKED = 16
-BATCH = 40
+BATCH = 120
 GROUP = 4
 AHEAD = 3
 CHUNK = 10
@@ -50,7 +50,7 @@
     return total + work[1, pl.ds(extra, rows), :]
 
 
-def kernel(n, width, gathers, strain_any, templates_any, profile_ref, overall_ref,
+def kernel(n, width, gathers, strain_any, templates_any, both_ref,
            strain_ref, templates_ref, halo, gathered, longer, work, near, hankel, sums, scales, minima, mine,
            local, halo_send, halo_recv, send, recv, out_send, out_recv):
     me = lax.axis_index("seg")
@@ -203,7 +203,7 @@
         each(n - 1, lambda step: template_copy(step).wait_send())
     rho = jnp.max(best.T, axis=0, keepdims=True)
     distance = jnp.sqrt(jnp.maximum(2.0 - 2.0 * rho, 0.0))
-    profile_ref[...] = distance
+    both_ref[pl.ds(0, 1), :] = distance
     mine[...] = distance
     minima[me] = distance
 
@@ -222,7 +222,7 @@
     each(n - 1, lambda step: out_copy(step).start())
     each(n - 1, lambda step: out_arrival(other(step)).wait_recv())
     each(n - 1, lambda step: out_copy(step).wait_send())
-    overall_ref[...] = jnp.min(minima[...], axis=0)
+    both_ref[pl.ds(1, 1), :] = jnp.min(minima[...], axis=0)
 
 
 def per_device(n, strain, templates):
@@ -236,11 +236,11 @@
     extra = width // LANES
     dma = pltpu.SemaphoreType.DMA
     vmem = pl.BlockSpec(memory_space=pltpu.VMEM)
-    profile, overall = pl.pallas_call(
+    both = pl.pallas_call(
         functools.partial(kernel, n, width, gathers),
-        out_shape=[pltpu.VMEM((1, queries), jnp.float32)] * 2,
+        out_shape=pltpu.VMEM((2, queries), jnp.float32),
         in_specs=[pl.BlockSpec(memory_space=pl.ANY)] * 2,
-        out_specs=[vmem] * 2,
+        out_specs=vmem,
         scratch_shapes=[
             pltpu.VMEM((rows, LANES), jnp.bfloat16),
             pltpu.VMEM(templates.shape, jnp.bfloat16),
@@ -258,7 +258,7 @@
         ],
         compiler_params=pltpu.CompilerParams(collective_id=0, has_side_effects=True),
     )(strain.reshape(rows, LANES), templates)
-    return (profile, overall.reshape(-1))
+    return (both[:1], both[1])
 
 
 def solution(mesh):

time: 20.5 us -> 19.4 us (0.946)
  Pallas kernels: 18.6 us -> 18.1 us
  local copies, waits for them, and re-layouts: 1.02 us -> 0.52 us
    unnamed x2 -> x0, local copies, waits for them, and re-layouts: 1.02 us -> none
    pallas_call x1, Pallas kernels: 18.6 us -> 18.1 us  [per_device(): pl.pallas_call(functools.partial(kernel, n, width, gathers), out_shape=pl...]
    squeeze x0 -> x1, local copies, waits for them, and re-layouts: none -> 0.52 us  [per_device(): return (both[:1], both[1])]
where the time goes in v5:
time: 19.4 us; the launch traced here: 19.2 us
  Pallas kernels  18.1 us (93%)
  between operations  0.64 us (3%)
  local copies, waits for them, and re-layouts  0.52 us (3%)
    pallas_call x1, Pallas kernels, per_device(): pl.pallas_call(functools.partial(kernel, n, width, gathers), out_shape=pl...  18.1 us
    squeeze x1, local copies, waits for them, and re-layouts, per_device(): return (both[:1], both[1])  0.52 us

profile of v5, /device:TPU:0, one launch (start us, length us, event | category | flops | bytes accessed | tf_op | source)
XLA Modules:
  0.0 19.2 jit_solution(4095195830936261638)
XLA Ops:
  0.6 18.1 %shard_map.41 = f32[2,128]{1,0:T(2,128)S(1)} custom-call(bf16[128,128]{1,0:T(8,128)(2,1)} %bitcast.3, bf16[8,512]{1,0:T(8,128)(2,1)} %templates_any.1), custom_call_target="tpu_custom_call" | custom-call | tf_op jit(solution)/shard_map/pallas_call | solution.py:239
  18.7 0.5 %slice_bitcast_fusion = (f32[128]{0:T(128)}, f32[1,128]{1,0:T(1,128)}) fusion(f32[2,128]{1,0:T(2,128)S(1)} %shard_map.41), kind=kLoop, calls=%fused_computation | loop fusion | bytes 2048 | tf_op jit(solution)/shard_map/squeeze | solution.py:261
